TPU v7x, 32 devices: a whole 2x2x4 slice. The times are simulated.
32 devices in a mesh: lon: 8 (over y, x, core), lat: 4 (over z).
Axes of the slice: x: 2, y: 2, z: 4, core: 2. Of those that a mesh axis runs over, the one named last changes fastest.
Arguments:
- u_wind: float32 [256, 192, 1024], P(None, 'lat', 'lon'), may hold values from -40 to 40
- v_wind: float32 [256, 192, 1024], P(None, 'lat', 'lon'), may hold values from -40 to 40
Outputs:
- eof_basis: float32 [256, 2, 192, 1024], P(None, None, 'lat', 'lon')
- r_factor: float32 [256, 256], replicated
All inputs are finite; a program needn't handle non-finite values.
Results may differ from a plain program's by a relative error of at most 0.00022.
Values sent between devices are 32-bit elements; how exact they have to be, the bound alone decides.
No kernel may reach another device: no remote copies, remote signals or barrier semaphores. Data moves between devices by JAX's collectives and lax.ppermute only.
A program may use at most 256 MiB of HBM per device.

v0:
```python
import jax
import jax.numpy as jnp
from jax import lax
from jax.sharding import PartitionSpec as P


def extended(cells, sides, width, closed):
    for axis, dim in sides:
        count = lax.axis_size(axis)
        ends = count if closed else count - 1
        head = lax.slice_in_dim(cells, 0, width, axis=dim)
        tail = lax.slice_in_dim(cells, cells.shape[dim] - width, cells.shape[dim], axis=dim)
        cells = jnp.concatenate(
            [
                lax.ppermute(tail, axis, [(i, (i + 1) % count) for i in range(ends)]),
                cells,
                lax.ppermute(head, axis, [((i + 1) % count, i) for i in range(ends)]),
            ],
            axis=dim,
        )
    return cells


def centred(padded, axis, count):

    def piece(lower):
        return lax.slice_in_dim(padded, lower, lower + count, axis=axis)

    return (8.0 * (piece(3) - piece(1)) - (piece(4) - piece(0))) / 12.0


def cross(left, right):
    return lax.dot_general(
        left,
        right,
        (((1,), (1,)), ((), ())),
        precision=lax.Precision.HIGHEST,
        preferred_element_type=jnp.float32,
    )


def summed_parts(parts):
    shares = (lax.psum_scatter(parts[0], "lon", scatter_dimension=0, tiled=True),)
    shares = lax.psum((shares[0],), "lat")
    return (lax.all_gather(shares[0], "lon", axis=0, tiled=True),)


def on_device(u_wind, v_wind):
    snaps, lat_rows, lon_cols = u_wind.shape
    n_lat = lat_rows * lax.axis_size("lat")
    n_lon = lon_cols * lax.axis_size("lon")
    ratio = n_lon / (2.0 * n_lat)
    winds = jnp.stack([u_wind, v_wind])
    lon_padded = extended(winds, (("lon", 3),), 2, True)
    lat_padded = extended(winds, (("lat", 2),), 2, False)
    global_rows = (lax.axis_index("lat") * lat_rows + jnp.arange(-2, lat_rows + 2)).astype(
        jnp.float32
    )
    phi = -jnp.pi / 2 + (global_rows + 0.5) * jnp.pi / n_lat
    cosine = jnp.cos(phi)
    root = jnp.sqrt(cosine[2:-2])[:, None]
    along_lon = centred(lon_padded, 3, lon_cols)
    along_lat = centred(lat_padded * cosine[None, None, :, None], 2, lat_rows)
    zeta = (ratio * along_lon[1] - along_lat[0]) / root
    delta = (ratio * along_lon[0] + along_lat[1]) / root
    matrix = jnp.stack([zeta, delta], axis=1).reshape(snaps, -1)
    total = 2.0 * n_lat * n_lon
    gram = summed_parts((cross(matrix, matrix),))[0]
    gram = gram / total
    lower = jnp.linalg.cholesky(gram)
    inverse = jax.scipy.linalg.solve_triangular(
        lower, jnp.eye(snaps, dtype=jnp.float32), lower=True
    )
    basis = jnp.dot(
        inverse, matrix, precision=lax.Precision.HIGHEST, preferred_element_type=jnp.float32
    )
    return (basis.reshape(snaps, 2, lat_rows, lon_cols), lower.T)


def solution(mesh):
    in_specs = (P(None, "lat", "lon"), P(None, "lat", "lon"))
    out_specs = (P(None, None, "lat", "lon"), P())
    return jax.shard_map(
        on_device, mesh=mesh, in_specs=in_specs, out_specs=out_specs, check_vma=False
    )
```

profile of v0, /device:TPU:0, one launch (start us, length us, event | category | flops | bytes accessed | tf_op | source)
XLA Modules:
  0.0 353.5 jit_solution(14856567004534644817)
XLA Ops:
  7.2 10.9 %copy_bitcast_fusion = (f32[1,256,48,128]{3,1,2,0:T(8,128)S(1)}, f32[1,256,48,128]{3,1,2,0:T(8,128)}) fusion(f32[256,48,128]{2,1,0:T(8,128)} %param.3, f32[256,48,128]{2,1,0:T(8,128)} %param.2), kind=kLoop, calls=%fused_computation.34 | loop fusion | bytes 25165824 | tf_op jit(solution)/shard_map/stack | solution.py:53
  18.1 16.8 %fusion = (f32[2,256,48,2]{3,1,2,0:T(8,128)}, f32[2,256,48,2]{3,1,2,0:T(8,128)}) fusion(f32[1,256,48,128]{3,1,2,0:T(8,128)} %get-tuple-element.43, f32[1,256,48,128]{3,1,2,0:T(8,128)S(1)} %get-tuple-element.42), kind=kLoop, calls=%fused_computation.11 | loop fusion | flops 98304 | bytes 12976128 | tf_op jit(solution)/shard_map/stack | solution.py:53
  35.0 7.6 %copy.19 = f32[2,256,48,2]{1,2,3,0:T(8,128)S(1)} copy(f32[2,256,48,2]{3,1,2,0:T(8,128)} %get-tuple-element.30) | data formatting | bytes 393216 | tf_op jit(solution)/shard_map/slice | solution.py:11
  42.6 3.4 collective-permute-start
  46.0 7.6 %copy.21 = f32[2,256,48,2]{1,2,3,0:T(8,128)S(1)} copy(f32[2,256,48,2]{3,1,2,0:T(8,128)} %get-tuple-element.31) | data formatting | bytes 393216 | tf_op jit(solution)/shard_map/slice | solution.py:12
  53.6 1.3 fusion.14
  54.9 3.5 collective-permute-start.2
  58.4 1.8 collective-permute-start.3
  60.3 0.1 slice_sqrt_fusion
  60.4 6.6 %copy.20 = f32[2,256,48,2]{3,1,2,0:T(8,128)} copy(f32[2,256,48,2]{1,2,3,0:T(8,128)S(1)} %collective-permute-done) | data formatting | bytes 393216 | tf_op jit(solution)/shard_map/ppermute | solution.py:17
  66.9 6.6 %copy.22 = f32[2,256,48,2]{3,1,2,0:T(8,128)} copy(f32[2,256,48,2]{1,2,3,0:T(8,128)S(1)} %collective-permute-done.1) | data formatting | bytes 393216 | tf_op jit(solution)/shard_map/ppermute | solution.py:15
  73.5 33.8 %pad_maximum_fusion = (f32[2,256,48,130]{3,1,2,0:T(8,128)}, f32[2,256,48,130]{3,1,2,0:T(8,128)}) fusion(f32[2,256,48,2]{3,1,2,0:T(8,128)} %copy.20, f32[1,256,48,128]{3,1,2,0:T(8,128)} %copy-done, f32[1,256,48,128]{3,1,2,0:T(8,128)} %get-tuple-element.43, f32[2,256,48,2]{3,1,2,0:T(8,128)} %copy.22), kind=kLoop, calls=%fused_computation.2 | loop fusion | flops 12779520 | bytes 38535168 | tf_op jit(solution)/shard_map/concatenate | solution.py:13
  107.3 36.6 %fusion.6 = f32[2,256,48,128]{3,1,2,0:T(8,128)} fusion(f32[2,256,48,130]{3,1,2,0:T(8,128)} %get-tuple-element.29, f32[2,256,48,130]{3,1,2,0:T(8,128)} %get-tuple-element.28), kind=kLoop, calls=%fused_computation.20 | loop fusion | flops 15728640 | bytes 62914560 | tf_op jit(solution)/shard_map/div | solution.py:29
  143.9 5.7 %maximum_multiply_fusion = f32[2,256,52,128]{3,1,2,0:T(8,128)S(1)} fusion(f32[2,256,2,128]{3,1,2,0:T(8,128)} %collective-permute-done.3, f32[1,256,48,128]{3,1,2,0:T(8,128)} %copy-done, f32[1,256,48,128]{3,1,2,0:T(8,128)} %get-tuple-element.43, f32[2,256,2,128]{3,1,2,0:T(8,128)S(1)} %collective-permute-done.2, f32[52]{0:T(128)S(1)} %add_cosine_fusion), kind=kLoop, calls=%fused_computation.10 | loop fusion | flops 13631488 | bytes 27263184 | tf_op jit(solution)/shard_map/mul | solution.py:63
  149.7 7.5 %fusion.3 = f32[2,256,48,128]{3,1,2,0:T(8,128)} fusion(f32[2,256,52,128]{3,1,2,0:T(8,128)S(1)} %maximum_multiply_fusion), kind=kLoop, calls=%fused_computation.15 | loop fusion | flops 15728640 | bytes 62914560 | tf_op jit(solution)/shard_map/div | solution.py:29
  157.1 9.7 %fusion.13 = (f32[256,1,48,128]{3,0,2,1:T(8,128)S(1)}, f32[256,1,48,128]{3,0,2,1:T(8,128)S(1)}) fusion(f32[2,256,48,128]{3,1,2,0:T(8,128)} %fusion.3, f32[2,256,48,128]{3,1,2,0:T(8,128)} %fusion.6, f32[48]{0:T(128)S(1)} %slice_sqrt_fusion), kind=kLoop, calls=%fused_computation.32 | loop fusion | flops 9437184 | bytes 37748928 | tf_op jit(solution)/shard_map/div | solution.py:64
  166.8 2.6 copy-done.1
  169.4 1.9 copy-done.2
  171.3 12.4 %convolution_bitcast_fusion = f32[256,256]{1,0:T(8,128)} fusion(f32[256,1,48,128]{3,0,2,1:T(8,128)S(1)} %get-tuple-element.27, f32[256,1,48,128]{3,0,2,1:T(8,128)S(1)} %get-tuple-element.26), kind=kOutput, calls=%fused_computation.36 | convolution fusion | flops 9666822144 | bytes 12845056 | tf_op jit(solution)/shard_map/dot_general | solution.py:33
  183.7 10.9 %pad_maximum_fusion.1 = f32[256,2,48,128]{3,0,2,1:T(8,128)} fusion(f32[256,1,48,128]{3,0,2,1:T(8,128)} %copy-done.2, f32[256,1,48,128]{3,0,2,1:T(8,128)} %copy-done.1), kind=kLoop, calls=%fused_computation.23 | loop fusion | flops 3145728 | bytes 25165824 | tf_op jit(solution)/shard_map/stack | solution.py:66
  194.7 12.6 %copy.27 = f32[256,2,48,128]{0,3,2,1:T(8,128)} copy(f32[256,2,48,128]{3,0,2,1:T(8,128)} %pad_maximum_fusion.1) | data formatting | bytes 25165824 | tf_op jit(solution)/shard_map/stack | solution.py:66
  207.3 13.1 %reduce-scatter.4.cloned.1.call-done = f32[32,256]{1,0:T(8,128)} async-done(((f32[256,256]{1,0:T(8,128)}), f32[32,256]{1,0:T(8,128)}) %reduce-scatter.4.cloned.1.call-update) | async-done | bytes 32784
  220.4 0.9 copy.34
  221.2 21.1 %psum.7 = f32[32,256]{0,1:T(8,128)S(1)} all-reduce(f32[32,256]{0,1:T(8,128)S(1)} %copy.34), channel_id=1, replica_groups=mesh['lon'=8,'lat'=4] {'lat'}, use_global_device_ids=true, to_apply=%region_1.0 | all-reduce | flops 8192 | bytes 65536 | tf_op jit(solution)/shard_map/psum | solution.py:44
  242.3 0.1 copy.24
  242.4 9.6 %all_gather.3 = f32[256,256]{1,0:T(8,128)S(1)} all-gather(f32[32,256]{1,0:T(8,128)S(1)} %copy.24), channel_id=1, replica_groups=mesh['lon'=8,'lat'=4] {'lon'}, dimensions={0}, use_global_device_ids=true | all-gather | bytes 294912 | tf_op jit(solution)/shard_map/all_gather | solution.py:45
  252.0 0.1 copy.25
  252.1 0.1 copy.26
  252.3 11.7 %cholesky.50 = f32[128,128]{1,0:T(8,128)S(1)} custom-call(f32[128,128]{1,0:T(8,128)S(1)} %cholesky.118), custom_call_target="Cholesky" | custom-call | tf_op jit(solution)/shard_map/jit(cholesky)/cholesky | solution.py:70
  264.1 9.8 %custom-call.15 = f32[1,128,128]{1,2,0:T(8,128)S(1)} custom-call(f32[1,128,128]{2,1,0:T(8,128)S(1)} %get-tuple-element.39), custom_call_target="InvertDiagBlocksLowerTriangular" | custom-call | tf_op jit(solution)/shard_map/jit(cholesky)/cholesky | solution.py:70
  273.9 0.2 constant_dynamic-update-slice_fusion.1
  274.1 0.3 convolution_subtract_fusion.1
  274.4 11.7 %cholesky.105 = f32[128,128]{1,0:T(8,128)S(1)} custom-call(f32[128,128]{1,0:T(8,128)S(1)} %convolution_subtract_fusion.1), custom_call_target="Cholesky" | custom-call | tf_op jit(solution)/shard_map/jit(cholesky)/cholesky | solution.py:70
  286.1 0.6 compare_reduce_fusion
  286.8 0.6 compare_reduce_fusion.1
  288.8 0.1 triangular_solve.63
  288.8 4.2 %while.1 = (s32[]{:T(128)}, f32[256,256]{1,0:T(8,128)S(1)}, s32[2,2]{1,0:T(2,128)S(1)}, f32[2,128,128]{2,1,0:T(8,128)S(1)}, s32[]{:T(128)}) while((s32[]{:T(128)}, f32[256,256]{1,0:T(8,128)S(1)}, s32[2,2]{1,0:T(2,128)S(1)}, f32[2,128,128]{2,1,0:T(8,128)S(1)}, s32[]{:T(128)}) %tuple.35), condition=%wide.while_cond, body=%wide.while_body.sunk | while | flops 2 | bytes 131181 | solution.py:71
  289.0 0.6 fusion.34
  289.6 1.4 bitcast_dynamic-update-slice_fusion.2
  291.0 0.6 fusion.34
  291.6 1.4 bitcast_dynamic-update-slice_fusion.2
  293.0 19.7 %custom-call.16 = f32[2,128,128]{1,2,0:T(8,128)S(1)} custom-call(f32[2,128,128]{2,1,0:T(8,128)S(1)} %get-tuple-element.9), custom_call_target="InvertDiagBlocksLowerTriangular" | custom-call | tf_op jit(solution)/shard_map/jit(_solve_triangular)/triangular_solve | solution.py:71
  312.7 0.3 fusion.20
  313.0 0.3 convolution_subtract_fusion
  313.3 0.3 fusion.23
  313.6 15.3 %fusion.8 = f32[256,2,48,128]{3,0,2,1:T(8,128)} fusion(f32[256,2,48,128]{0,3,2,1:T(8,128)} %copy.27, f32[128,256]{1,0:T(8,128)S(1)} %fusion.23, f32[128,256]{1,0:T(8,128)S(1)} %fusion.20), kind=kOutput, calls=%fused_computation.24 | convolution fusion | flops 9663741952 | bytes 25427968 | tf_op jit(solution)/shard_map/dot_general | solution.py:74
  328.9 16.6 %copy.28 = f32[256,2,48,128]{3,2,1,0:T(8,128)} copy(f32[256,2,48,128]{3,0,2,1:T(8,128)} %fusion.8) | data formatting | bytes 25165824
  345.5 0.8 copy.29
  (24 shorter events, 0.4 us)
Async XLA Ops:
  7.2 213.2 %reduce-scatter.4.cloned.1.call-start = ((), (), s32[]{:S(2)}) async-start(), calls=%async_computation.1 | async-start | bytes 294912
  18.1 16.8 %copy-start = (f32[1,256,48,128]{3,1,2,0:T(8,128)}, f32[1,256,48,128]{3,1,2,0:T(8,128)S(1)}, u32[]{:S(2)}) copy-start(f32[1,256,48,128]{3,1,2,0:T(8,128)S(1)} %get-tuple-element.42) | copy-start | bytes 18874372
  42.6 17.8 %collective-permute-start = (f32[2,256,48,2]{1,2,3,0:T(8,128)S(1)}, f32[2,256,48,2]{1,2,3,0:T(8,128)S(1)}, u32[]{:S(2)}, u32[]{:S(2)}) collective-permute-start(f32[2,256,48,2]{1,2,3,0:T(8,128)S(1)} %copy.19), channel_id=1, source_target_pairs={{4,0},{8,4},{12,8},{16,12},{20,16},{24,20},{28,24},{0,28},{5,1},{9... | collective-permute-start | bytes 589832 | tf_op jit(solution)/shard_map/ppermute | solution.py:17
  53.5 13.4 %collective-permute-start.1 = (f32[2,256,48,2]{1,2,3,0:T(8,128)S(1)}, f32[2,256,48,2]{1,2,3,0:T(8,128)S(1)}, u32[]{:S(2)}, u32[]{:S(2)}) collective-permute-start(f32[2,256,48,2]{1,2,3,0:T(8,128)S(1)} %copy.21), channel_id=1, source_target_pairs={{0,4},{4,8},{8,12},{12,16},{16,20},{20,24},{24,28},{28,0},{1,5},{5... | collective-permute-start | bytes 589832 | tf_op jit(solution)/shard_map/ppermute | solution.py:15
  54.9 89.0 %collective-permute-start.2 = (f32[2,256,2,128]{3,1,2,0:T(8,128)S(1)}, f32[2,256,2,128]{3,1,2,0:T(8,128)S(1)}, u32[]{:S(2)}, u32[]{:S(2)}) collective-permute-start(f32[2,256,2,128]{3,1,2,0:T(8,128)S(1)} %get-tuple-element.32), channel_id=1, source_target_pairs={{0,1},{1,2},{2,3},{4,5},{5,6},{6,7},{8,9},{9,10},{10,11},{12,13},{... | collective-permute-start | bytes 1572872 | tf_op jit(solution)/shard_map/ppermute | solution.py:15
  58.4 85.5 %collective-permute-start.3 = (f32[2,256,2,128]{3,1,2,0:T(8,128)S(1)}, f32[2,256,2,128]{3,1,2,0:T(8,128)}, u32[]{:S(2)}, u32[]{:S(2)}) collective-permute-start(f32[2,256,2,128]{3,1,2,0:T(8,128)S(1)} %get-tuple-element.33), channel_id=1, source_target_pairs={{1,0},{2,1},{3,2},{5,4},{6,5},{7,6},{9,8},{10,9},{11,10},{13,12},{... | collective-permute-start | bytes 1572872 | tf_op jit(solution)/shard_map/ppermute | solution.py:17
  166.8 2.7 copy-start.1
  166.8 4.5 %copy-start.2 = (f32[256,1,48,128]{3,0,2,1:T(8,128)}, f32[256,1,48,128]{3,0,2,1:T(8,128)S(1)}, u32[]{:S(2)}) copy-start(f32[256,1,48,128]{3,0,2,1:T(8,128)S(1)} %get-tuple-element.27) | copy-start | bytes 18874372
Sparse Core Ops, SparseCore 0:
  183.9 36.4 reduce-scatter.3
where the time goes:
time: 359 us; the launch traced here: 353 us
  other arithmetic  177 us (49%)
  local copies, waits for them, and re-layouts  79.1 us (22%)
  blocking collectives  30.7 us (9%)
  matrix products  29 us (8%)
  between operations  15.8 us (4%)
  waiting for transfers between devices  13.1 us (4%)
  starting transfers between devices  8.78 us (2%)
    div x2, other arithmetic, centred(): return (8.0 * (piece(3) - piece(1)) - (piece(4) - piece(0))) / 12.0  44.1 us
    another operation x7, other arithmetic, on_device(): lower = jnp.linalg.cholesky(gram)  34.6 us
    concatenate x1, other arithmetic, extended(): jnp.concatenate([lax.ppermute(tail, axis, [(i, (i + 1) % count) for i in...  33.8 us
    unnamed x9, local copies, waits for them, and re-layouts  22.8 us
    psum x1, blocking collectives, summed_parts(): shares = lax.psum((shares[0],), 'lat')  21.1 us
    another operation x2, other arithmetic, on_device(): jax.scipy.linalg.solve_triangular(lower, jnp.eye(snaps, dtype=jnp.float32...  19.7 us
    another operation x2, other arithmetic, on_device(): winds = jnp.stack([u_wind, v_wind])  18.1 us
    dot_general x1, matrix products, on_device(): jnp.dot(inverse, matrix, precision=lax.Precision.HIGHEST, preferred_eleme...  15.3 us
  transfers between devices with their start and end apart: 5, of which 1 were waited for; matrix products, arithmetic and copies ran while one was open for 33% of the time, Pallas kernels for 0%

commit v1 on v0

--- a/solution.py
+++ b/solution.py
@@ -42,7 +42,11 @@
 def summed_parts(parts):
     shares = (lax.psum_scatter(parts[0], "lon", scatter_dimension=0, tiled=True),)
     shares = lax.psum((shares[0],), "lat")
-    return (lax.all_gather(shares[0], "lon", axis=0, tiled=True),)
+    return (
+        jnp.concatenate(
+            lax.all_to_all(jnp.stack([shares[0]] * lax.axis_size("lon")), "lon", 0, 0), axis=0
+        ),
+    )
 
 
 def on_device(u_wind, v_wind):

time: 359 us -> 375 us (1.045)
  waiting for transfers between devices: 13.1 us -> 36.6 us
  blocking collectives: 30.7 us -> 19.6 us
    reduce_scatter x0 -> x1, waiting for transfers between devices: none -> 36.6 us  [summed_parts(): lax.psum_scatter(parts[0], 'lon', scatter_dimension=0, tiled=True)]
    unnamed x2 -> x1, waiting for transfers between devices: 13.1 us -> 0.02 us
    all_gather x1 -> x0, blocking collectives: 9.59 us -> none  [summed_parts(): return (lax.all_gather(shares[0], 'lon', axis=0, tiled=True),)]
    unnamed x9 -> x8, local copies, waits for them, and re-layouts: 22.8 us -> 22 us
  transfers between devices with their start and end apart: 5 -> 6, of which waited for: 1 -> 1; matrix products, arithmetic and copies ran while one was open for 33% -> 31% of each run, Pallas kernels for 0% -> 0%
where the time goes in v1:
time: 375 us; the launch traced here: 369 us
  other arithmetic  177 us (47%)
  local copies, waits for them, and re-layouts  78.8 us (21%)
  waiting for transfers between devices  36.6 us (10%)
  matrix products  28.8 us (8%)
  blocking collectives  19.6 us (5%)
  between operations  15.8 us (4%)
  starting transfers between devices  12.4 us (3%)
    div x2, other arithmetic, centred(): return (8.0 * (piece(3) - piece(1)) - (piece(4) - piece(0))) / 12.0  44.1 us
    reduce_scatter x1, waiting for transfers between devices, summed_parts(): lax.psum_scatter(parts[0], 'lon', scatter_dimension=0, tiled=True)  36.6 us
    another operation x7, other arithmetic, on_device(): lower = jnp.linalg.cholesky(gram)  34.6 us
    concatenate x1, other arithmetic, extended(): jnp.concatenate([lax.ppermute(tail, axis, [(i, (i + 1) % count) for i in...  33.9 us
    unnamed x8, local copies, waits for them, and re-layouts  22 us
    another operation x2, other arithmetic, on_device(): jax.scipy.linalg.solve_triangular(lower, jnp.eye(snaps, dtype=jnp.float32...  19.9 us
    psum x1, blocking collectives, summed_parts(): shares = lax.psum((shares[0],), 'lat')  19.6 us
    another operation x2, other arithmetic, on_device(): winds = jnp.stack([u_wind, v_wind])  18.1 us
  transfers between devices with their start and end apart: 6, of which 1 were waited for; matrix products, arithmetic and copies ran while one was open for 31% of the time, Pallas kernels for 0%

profile of v1, /device:TPU:0, one launch (start us, length us, event | category | flops | bytes accessed | tf_op | source)
XLA Modules:
  0.0 369.0 jit_solution(1985121883274374150)
XLA Ops:
  7.2 0.0 reduce-scatter.2.cloned.1.call-start
  7.2 10.9 %copy_bitcast_fusion = (f32[1,256,48,128]{3,1,2,0:T(8,128)S(1)}, f32[1,256,48,128]{3,1,2,0:T(8,128)}) fusion(f32[256,48,128]{2,1,0:T(8,128)} %param.3, f32[256,48,128]{2,1,0:T(8,128)} %param.2), kind=kLoop, calls=%fused_computation.34 | loop fusion | bytes 25165824 | tf_op jit(solution)/shard_map/stack | solution.py:57
  18.1 16.8 %fusion = (f32[2,256,48,2]{3,1,2,0:T(8,128)}, f32[2,256,48,2]{3,1,2,0:T(8,128)}) fusion(f32[1,256,48,128]{3,1,2,0:T(8,128)} %get-tuple-element.43, f32[1,256,48,128]{3,1,2,0:T(8,128)S(1)} %get-tuple-element.42), kind=kLoop, calls=%fused_computation.11 | loop fusion | flops 98304 | bytes 12976128 | tf_op jit(solution)/shard_map/stack | solution.py:57
  35.0 7.6 %copy.18 = f32[2,256,48,2]{1,2,3,0:T(8,128)S(1)} copy(f32[2,256,48,2]{3,1,2,0:T(8,128)} %get-tuple-element.30) | data formatting | bytes 393216 | tf_op jit(solution)/shard_map/slice | solution.py:11
  42.6 3.4 collective-permute-start
  46.0 7.6 %copy.20 = f32[2,256,48,2]{1,2,3,0:T(8,128)S(1)} copy(f32[2,256,48,2]{3,1,2,0:T(8,128)} %get-tuple-element.31) | data formatting | bytes 393216 | tf_op jit(solution)/shard_map/slice | solution.py:12
  53.5 0.1 collective-permute-start.1
  53.6 1.3 fusion.14
  54.9 3.5 collective-permute-start.2
  58.4 1.8 collective-permute-start.3
  60.2 0.1 slice_sqrt_fusion
  60.3 6.6 %copy.19 = f32[2,256,48,2]{3,1,2,0:T(8,128)} copy(f32[2,256,48,2]{1,2,3,0:T(8,128)S(1)} %collective-permute-done) | data formatting | bytes 393216 | tf_op jit(solution)/shard_map/ppermute | solution.py:17
  66.9 6.6 %copy.21 = f32[2,256,48,2]{3,1,2,0:T(8,128)} copy(f32[2,256,48,2]{1,2,3,0:T(8,128)S(1)} %collective-permute-done.1) | data formatting | bytes 393216 | tf_op jit(solution)/shard_map/ppermute | solution.py:15
  73.5 33.9 %pad_maximum_fusion = (f32[2,256,48,130]{3,1,2,0:T(8,128)}, f32[2,256,48,130]{3,1,2,0:T(8,128)}) fusion(f32[2,256,48,2]{3,1,2,0:T(8,128)} %copy.19, f32[1,256,48,128]{3,1,2,0:T(8,128)} %copy-done, f32[1,256,48,128]{3,1,2,0:T(8,128)} %get-tuple-element.43, f32[2,256,48,2]{3,1,2,0:T(8,128)} %copy.21), kind=kLoop, calls=%fused_computation.2 | loop fusion | flops 12779520 | bytes 38535168 | tf_op jit(solution)/shard_map/concatenate | solution.py:13
  107.3 36.6 %fusion.6 = f32[2,256,48,128]{3,1,2,0:T(8,128)} fusion(f32[2,256,48,130]{3,1,2,0:T(8,128)} %get-tuple-element.29, f32[2,256,48,130]{3,1,2,0:T(8,128)} %get-tuple-element.28), kind=kLoop, calls=%fused_computation.20 | loop fusion | flops 15728640 | bytes 62914560 | tf_op jit(solution)/shard_map/div | solution.py:29
  144.0 5.7 %maximum_multiply_fusion = f32[2,256,52,128]{3,1,2,0:T(8,128)S(1)} fusion(f32[2,256,2,128]{3,1,2,0:T(8,128)} %collective-permute-done.3, f32[1,256,48,128]{3,1,2,0:T(8,128)} %copy-done, f32[1,256,48,128]{3,1,2,0:T(8,128)} %get-tuple-element.43, f32[2,256,2,128]{3,1,2,0:T(8,128)S(1)} %collective-permute-done.2, f32[52]{0:T(128)S(1)} %add_cosine_fusion), kind=kLoop, calls=%fused_computation.10 | loop fusion | flops 13631488 | bytes 27263184 | tf_op jit(solution)/shard_map/mul | solution.py:67
  149.7 7.5 %fusion.3 = f32[2,256,48,128]{3,1,2,0:T(8,128)} fusion(f32[2,256,52,128]{3,1,2,0:T(8,128)S(1)} %maximum_multiply_fusion), kind=kLoop, calls=%fused_computation.15 | loop fusion | flops 15728640 | bytes 62914560 | tf_op jit(solution)/shard_map/div | solution.py:29
  157.2 9.7 %fusion.13 = (f32[256,1,48,128]{3,0,2,1:T(8,128)S(1)}, f32[256,1,48,128]{3,0,2,1:T(8,128)S(1)}) fusion(f32[2,256,48,128]{3,1,2,0:T(8,128)} %fusion.3, f32[2,256,48,128]{3,1,2,0:T(8,128)} %fusion.6, f32[48]{0:T(128)S(1)} %slice_sqrt_fusion), kind=kLoop, calls=%fused_computation.32 | loop fusion | flops 9437184 | bytes 37748928 | tf_op jit(solution)/shard_map/div | solution.py:68
  166.9 2.6 copy-done.1
  169.5 1.9 copy-done.2
  171.4 12.4 %convolution_bitcast_fusion = f32[256,256]{1,0:T(8,128)} fusion(f32[256,1,48,128]{3,0,2,1:T(8,128)S(1)} %get-tuple-element.27, f32[256,1,48,128]{3,0,2,1:T(8,128)S(1)} %get-tuple-element.26), kind=kOutput, calls=%fused_computation.36 | convolution fusion | flops 9666822144 | bytes 12845056 | tf_op jit(solution)/shard_map/dot_general | solution.py:33
  183.9 36.6 %reduce-scatter.2.cloned.1.call-done = f32[32,256]{1,0:T(8,128)} async-done(((f32[256,256]{1,0:T(8,128)}), f32[32,256]{1,0:T(8,128)}) %reduce-scatter.2.cloned.1.call-update) | async-done | bytes 32784 | tf_op jit(solution)/shard_map/reduce_scatter | solution.py:43
  220.4 19.6 %psum.7 = f32[32,256]{1,0:T(8,128)S(1)} all-reduce(f32[32,256]{1,0:T(8,128)} %reduce-scatter.2.cloned.1.call-done), channel_id=1, replica_groups=mesh['lon'=8,'lat'=4] {'lat'}, use_global_device_ids=true, to_apply=%region_1.0 | all-reduce | flops 8192 | bytes 65536 | tf_op jit(solution)/shard_map/psum | solution.py:44
  240.0 0.7 stack.14
  240.7 3.6 all-to-all-start
  244.3 10.9 %pad_maximum_fusion.1 = f32[256,2,48,128]{3,0,2,1:T(8,128)} fusion(f32[256,1,48,128]{3,0,2,1:T(8,128)} %copy-done.2, f32[256,1,48,128]{3,0,2,1:T(8,128)} %copy-done.1), kind=kLoop, calls=%fused_computation.23 | loop fusion | flops 3145728 | bytes 25165824 | tf_op jit(solution)/shard_map/stack | solution.py:70
  255.3 12.6 %copy.23 = f32[256,2,48,128]{0,3,2,1:T(8,128)} copy(f32[256,2,48,128]{3,0,2,1:T(8,128)} %pad_maximum_fusion.1) | data formatting | bytes 25165824 | tf_op jit(solution)/shard_map/stack | solution.py:70
  267.9 0.1 copy.22
  268.1 11.7 %cholesky.50 = f32[128,128]{1,0:T(8,128)S(1)} custom-call(f32[128,128]{1,0:T(8,128)S(1)} %cholesky.118), custom_call_target="Cholesky" | custom-call | tf_op jit(solution)/shard_map/jit(cholesky)/cholesky | solution.py:74
  279.9 9.8 %custom-call.15 = f32[1,128,128]{1,2,0:T(8,128)S(1)} custom-call(f32[1,128,128]{2,1,0:T(8,128)S(1)} %get-tuple-element.39), custom_call_target="InvertDiagBlocksLowerTriangular" | custom-call | tf_op jit(solution)/shard_map/jit(cholesky)/cholesky | solution.py:74
  289.7 0.2 constant_dynamic-update-slice_fusion.1
  289.9 0.3 convolution_subtract_fusion.1
  290.1 11.7 %cholesky.105 = f32[128,128]{1,0:T(8,128)S(1)} custom-call(f32[128,128]{1,0:T(8,128)S(1)} %convolution_subtract_fusion.1), custom_call_target="Cholesky" | custom-call | tf_op jit(solution)/shard_map/jit(cholesky)/cholesky | solution.py:74
  301.9 0.6 compare_reduce_fusion
  302.5 0.6 compare_reduce_fusion.1
  304.5 0.1 triangular_solve.63
  304.6 4.0 %while.1 = (s32[]{:T(128)}, f32[256,256]{1,0:T(8,128)S(1)}, s32[2,2]{1,0:T(2,128)S(1)}, f32[2,128,128]{2,1,0:T(8,128)S(1)}, s32[]{:T(128)}) while((s32[]{:T(128)}, f32[256,256]{1,0:T(8,128)S(1)}, s32[2,2]{1,0:T(2,128)S(1)}, f32[2,128,128]{2,1,0:T(8,128)S(1)}, s32[]{:T(128)}) %tuple.35), condition=%wide.while_cond, body=%wide.while_body.sunk | while | flops 2 | bytes 131181 | solution.py:75
  304.6 0.6 fusion.34
  305.2 1.4 bitcast_dynamic-update-slice_fusion.2
  306.6 0.6 fusion.34
  307.2 1.4 bitcast_dynamic-update-slice_fusion.2
  308.6 19.9 %custom-call.16 = f32[2,128,128]{1,2,0:T(8,128)S(1)} custom-call(f32[2,128,128]{2,1,0:T(8,128)S(1)} %get-tuple-element.9), custom_call_target="InvertDiagBlocksLowerTriangular" | custom-call | tf_op jit(solution)/shard_map/jit(_solve_triangular)/triangular_solve | solution.py:75
  328.5 0.3 fusion.20
  328.8 0.3 convolution_subtract_fusion
  329.0 0.3 fusion.23
  329.3 15.1 %fusion.8 = f32[256,2,48,128]{3,0,2,1:T(8,128)} fusion(f32[256,2,48,128]{0,3,2,1:T(8,128)} %copy.23, f32[128,256]{1,0:T(8,128)S(1)} %fusion.23, f32[128,256]{1,0:T(8,128)S(1)} %fusion.20), kind=kOutput, calls=%fused_computation.24 | convolution fusion | flops 9663741952 | bytes 25427968 | tf_op jit(solution)/shard_map/dot_general | solution.py:78
  344.4 16.6 %copy.24 = f32[256,2,48,128]{3,2,1,0:T(8,128)} copy(f32[256,2,48,128]{3,0,2,1:T(8,128)} %fusion.8) | data formatting | bytes 25165824
  361.1 0.8 copy.25
  (23 shorter events, 0.3 us)
Async XLA Ops:
  7.2 213.3 %reduce-scatter.2.cloned.1.call-start = ((), (), s32[]{:S(2)}) async-start(), calls=%async_computation.2 | async-start | bytes 294912 | tf_op jit(solution)/shard_map/reduce_scatter | solution.py:43
  18.1 16.8 %copy-start = (f32[1,256,48,128]{3,1,2,0:T(8,128)}, f32[1,256,48,128]{3,1,2,0:T(8,128)S(1)}, u32[]{:S(2)}) copy-start(f32[1,256,48,128]{3,1,2,0:T(8,128)S(1)} %get-tuple-element.42) | copy-start | bytes 18874372
  42.6 17.7 %collective-permute-start = (f32[2,256,48,2]{1,2,3,0:T(8,128)S(1)}, f32[2,256,48,2]{1,2,3,0:T(8,128)S(1)}, u32[]{:S(2)}, u32[]{:S(2)}) collective-permute-start(f32[2,256,48,2]{1,2,3,0:T(8,128)S(1)} %copy.18), channel_id=1, source_target_pairs={{4,0},{8,4},{12,8},{16,12},{20,16},{24,20},{28,24},{0,28},{5,1},{9... | collective-permute-start | bytes 589832 | tf_op jit(solution)/shard_map/ppermute | solution.py:17
  53.5 13.3 %collective-permute-start.1 = (f32[2,256,48,2]{1,2,3,0:T(8,128)S(1)}, f32[2,256,48,2]{1,2,3,0:T(8,128)S(1)}, u32[]{:S(2)}, u32[]{:S(2)}) collective-permute-start(f32[2,256,48,2]{1,2,3,0:T(8,128)S(1)} %copy.20), channel_id=1, source_target_pairs={{0,4},{4,8},{8,12},{12,16},{16,20},{20,24},{24,28},{28,0},{1,5},{5... | collective-permute-start | bytes 589832 | tf_op jit(solution)/shard_map/ppermute | solution.py:15
  54.9 89.1 %collective-permute-start.2 = (f32[2,256,2,128]{3,1,2,0:T(8,128)S(1)}, f32[2,256,2,128]{3,1,2,0:T(8,128)S(1)}, u32[]{:S(2)}, u32[]{:S(2)}) collective-permute-start(f32[2,256,2,128]{3,1,2,0:T(8,128)S(1)} %get-tuple-element.32), channel_id=1, source_target_pairs={{0,1},{1,2},{2,3},{4,5},{5,6},{6,7},{8,9},{9,10},{10,11},{12,13},{... | collective-permute-start | bytes 1572872 | tf_op jit(solution)/shard_map/ppermute | solution.py:15
  58.4 85.6 %collective-permute-start.3 = (f32[2,256,2,128]{3,1,2,0:T(8,128)S(1)}, f32[2,256,2,128]{3,1,2,0:T(8,128)}, u32[]{:S(2)}, u32[]{:S(2)}) collective-permute-start(f32[2,256,2,128]{3,1,2,0:T(8,128)S(1)} %get-tuple-element.33), channel_id=1, source_target_pairs={{1,0},{2,1},{3,2},{5,4},{6,5},{7,6},{9,8},{10,9},{11,10},{13,12},{... | collective-permute-start | bytes 1572872 | tf_op jit(solution)/shard_map/ppermute | solution.py:17
  166.8 2.6 copy-start.1
  166.8 4.5 %copy-start.2 = (f32[256,1,48,128]{3,0,2,1:T(8,128)}, f32[256,1,48,128]{3,0,2,1:T(8,128)S(1)}, u32[]{:S(2)}) copy-start(f32[256,1,48,128]{3,0,2,1:T(8,128)S(1)} %get-tuple-element.27) | copy-start | bytes 18874372
  240.7 27.1 %all-to-all-start = ((f32[8,32,256]{2,1,0:T(8,128)}), f32[8,32,256]{2,1,0:T(8,128)S(1)}, u32[]{:S(2)}, u32[]{:S(2)}) async-start(f32[8,32,256]{2,1,0:T(8,128)} %stack.14), calls=%async_computation.1 | async-start | bytes 524288 | tf_op jit(solution)/shard_map/all_to_all | solution.py:47
Sparse Core Ops, SparseCore 0:
  183.9 36.4 reduce-scatter.1
